TPU v7x, 32 devices: a whole 2x2x4 slice. The times are simulated.
32 devices in a mesh: rows: 16 (over z, x, core), feat: 2 (over y).
Axes of the slice: x: 2, y: 2, z: 4, core: 2. Of those that a mesh axis runs over, the one named last changes fastest.
Arguments:
- gradients: bfloat16 [16384, 8192], P('rows', 'feat'), may hold values from -2500 to 2500
- queries: bfloat16 [1024, 8192], P('rows', 'feat'), may hold values from -0.09375 to 0.09375
- loss_weight: float32 [16384], P('rows'), may hold values from 0.09 to 1
Outputs:
- standardized: bfloat16 [16384, 1024], P('rows', 'feat')
All inputs are finite; a program needn't handle non-finite values.
Results may differ from a plain program's by a relative error of at most 0.019.
Values may be sent and summed in bfloat16 or wider, within the bound.
No kernel may reach another device: no remote copies, remote signals or barrier semaphores. Data moves between devices by JAX's collectives and lax.ppermute only.
A program may use at most 64 MiB of HBM per device.

v0:
```python
import jax
import jax.numpy as jnp
from jax import lax
from jax.sharding import PartitionSpec as P

NORM_EPS = 1e-06
VAR_EPS = 1e-05


def body(gradients, queries, loss_weight):
    rows_here = gradients.shape[0]
    total_rows = rows_here * lax.axis_size("rows")
    feature_count = gradients.shape[1] * lax.axis_size("feat")
    local_squares = jnp.sum(jnp.square(gradients.astype(jnp.float32)), axis=1)
    squares = lax.psum(local_squares, "feat")
    product = lax.dot_general(
        gradients,
        lax.all_gather(queries, "rows", axis=0, tiled=True),
        (((1,), (1,)), ((), ())),
        preferred_element_type=jnp.float32,
    )
    partial_value = product.astype(jnp.bfloat16)
    partial_float = partial_value.astype(jnp.float32)
    raw = lax.psum_scatter(
        partial_float.astype(jnp.bfloat16), "feat", scatter_dimension=1, tiled=True
    ).astype(jnp.float32)
    factor = loss_weight / jnp.sqrt(squares / feature_count + NORM_EPS)
    scored = raw * factor[:, None]
    sums = lax.psum(jnp.sum(scored, axis=0), "rows")
    column_mean = sums / total_rows
    centered = scored - column_mean[None, :]
    square_sums = lax.psum(jnp.sum(centered * centered, axis=0), "rows")
    column_var = square_sums / total_rows
    return (centered * lax.rsqrt(column_var + VAR_EPS)[None, :]).astype(jnp.bfloat16)


def solution(mesh):
    in_specs = (P("rows", "feat"), P("rows", "feat"), P("rows"))
    out_specs = P("rows", "feat")
    return jax.shard_map(body, mesh=mesh, in_specs=in_specs, out_specs=out_specs, check_vma=False)
```

profile of v0, /device:TPU:0, one launch (start us, length us, event | category | flops | bytes accessed | tf_op | source)
XLA Modules:
  0.0 206.0 jit_solution(2264550643028440767)
XLA Ops:
  6.5 0.0 all-gather.2.cloned.1.call-start
  6.5 0.7 all-gather.2.cloned.1.call-update
  7.3 0.0 reduce-scatter.2.cloned.1.call-start
  7.3 79.2 %all-gather.2.cloned.1.call-done = bf16[1024,4096]{1,0:T(8,128)(2,1)} async-done(((bf16[64,4096]{1,0:T(8,128)(2,1)}), bf16[1024,4096]{1,0:T(8,128)(2,1)}) %all-gather.2.cloned.1.call-update) | async-done | bytes 8388624 | tf_op jit(solution)/shard_map/all_gather | solution.py:18
  86.5 14.7 %convolution_convert_fusion = bf16[1024,1024]{1,0:T(8,128)(2,1)} fusion(bf16[1024,4096]{1,0:T(8,128)(2,1)} %param.3, bf16[1024,4096]{1,0:T(8,128)(2,1)} %all-gather.2.cloned.1.call-done), kind=kOutput, calls=%fused_computation.6 | convolution fusion | flops 8590983168 | bytes 18874368 | tf_op jit(solution)/shard_map/dot_general | solution.py:16
  101.3 0.0 reduce-scatter.2.cloned.1.call-update
  101.3 0.0 copy-start.1
  101.3 5.1 %multiply_reduce_fusion = f32[1024]{0:T(1024)S(1)} fusion(bf16[1024,4096]{1,0:T(8,128)(2,1)} %param.3), kind=kLoop, calls=%fused_computation | loop fusion | flops 12581888 | bytes 8392704 | tf_op jit(solution)/shard_map/reduce_sum | solution.py:14
  106.4 5.1 %psum.21 = f32[1024]{0:T(1024)S(1)} all-reduce(f32[1024]{0:T(1024)S(1)} %multiply_reduce_fusion), channel_id=1, replica_groups=mesh['rows'=16,'feat'=2] {'feat'}, use_global_device_ids=true, to_apply=%region_2.0 | all-reduce | flops 1024 | bytes 8192 | tf_op jit(solution)/shard_map/psum | solution.py:15
  111.5 0.0 copy-done.1
  111.6 20.5 %reduce-scatter.2.cloned.1.call-done = bf16[1024,512]{1,0:T(8,128)(2,1)} async-done(((bf16[1024,1024]{1,0:T(8,128)(2,1)}), bf16[1024,512]{1,0:T(8,128)(2,1)}) %reduce-scatter.2.cloned.1.call-update) | async-done | bytes 1048592 | tf_op jit(solution)/shard_map/reduce_scatter | solution.py:24
  132.1 0.0 copy-start
  132.1 1.6 fusion.1
  133.7 33.0 %psum.22 = f32[512]{0:T(512)S(1)} all-reduce(f32[512]{0:T(512)S(1)} %fusion.1), channel_id=1, replica_groups=mesh['rows'=16,'feat'=2] {'rows'}, use_global_device_ids=true, to_apply=%region_4.0 | all-reduce | flops 512 | bytes 4096 | tf_op jit(solution)/shard_map/psum | solution.py:29
  166.7 1.6 multiply_reduce_fusion.1
  168.3 29.5 %psum.23 = f32[512]{0:T(512)S(1)} all-reduce(f32[512]{0:T(512)S(1)} %multiply_reduce_fusion.1), channel_id=1, replica_groups=mesh['rows'=16,'feat'=2] {'rows'}, use_global_device_ids=true, to_apply=%region_6.0 | all-reduce | flops 512 | bytes 4096 | tf_op jit(solution)/shard_map/psum | solution.py:32
  197.8 0.0 copy-done
  197.8 1.3 multiply_convert_fusion
  (3 shorter events, 0.0 us)
Async XLA Ops:
  6.5 80.0 %all-gather.2.cloned.1.call-start = ((), (), s32[]{:S(2)}) async-start(), calls=%async_computation.1 | async-start | bytes 8912896 | tf_op jit(solution)/shard_map/all_gather | solution.py:18
  7.3 124.8 %reduce-scatter.2.cloned.1.call-start = ((), (), s32[]{:S(2)}) async-start(), calls=%async_computation.2 | async-start | bytes 3145728 | tf_op jit(solution)/shard_map/reduce_scatter | solution.py:24
  101.3 10.2 %copy-start.1 = (f32[1024]{0:T(1024)S(1)}, f32[1024]{0:T(1024)}, u32[]{:S(2)}) copy-start(f32[1024]{0:T(1024)} %param.5) | copy-start | bytes 12292
  132.1 65.8 %copy-start = (bf16[1024,512]{1,0:T(8,128)(2,1)S(1)}, bf16[1024,512]{1,0:T(8,128)(2,1)}, u32[]{:S(2)}) copy-start(bf16[1024,512]{1,0:T(8,128)(2,1)} %reduce-scatter.2.cloned.1.call-done) | copy-start | bytes 3145732
Sparse Core Ops, SparseCore 0:
  9.5 77.0 all-gather.1
  101.4 30.5 reduce-scatter.1
where the time goes:
time: 206 us
  waiting for transfers between devices  100 us (49%)
  blocking collectives  67.7 us (33%)
  matrix products  14.7 us (7%)
  between operations  13.4 us (7%)
  other arithmetic  9.68 us (5%)
    all_gather x1, waiting for transfers between devices, body(): lax.all_gather(queries, 'rows', axis=0, tiled=True)  79.2 us
    psum x1, blocking collectives, body(): sums = lax.psum(jnp.sum(scored, axis=0), 'rows')  33 us
    psum x1, blocking collectives, body(): square_sums = lax.psum(jnp.sum(centered * centered, axis=0), 'rows')  29.5 us
    reduce_scatter x1, waiting for transfers between devices, body(): lax.psum_scatter(partial_float.astype(jnp.bfloat16), 'feat', scatter_dime...  20.5 us
    dot_general x1, matrix products, body(): lax.dot_general(gradients, lax.all_gather(queries, 'rows', axis=0, tiled=...  14.7 us
    psum x1, blocking collectives, body(): squares = lax.psum(local_squares, 'feat')  5.15 us
    reduce_sum x1, other arithmetic, body(): local_squares = jnp.sum(jnp.square(gradients.astype(jnp.float32)), axis=1)  5.08 us
  transfers between devices with their start and end apart: 2, of which 2 were waited for; matrix products, arithmetic and copies ran while one was open for 2% of the time, Pallas kernels for 0%

commit v1 on v0

--- a/solution.py
+++ b/solution.py
@@ -29,7 +29,7 @@
     sums = lax.psum(jnp.sum(scored, axis=0), "rows")
     column_mean = sums / total_rows
     centered = scored - column_mean[None, :]
-    square_sums = lax.psum(jnp.sum(centered * centered, axis=0), "rows")
+    square_sums = jnp.sum(lax.all_gather(jnp.sum(centered * centered, axis=0), "rows"), axis=0)
     column_var = square_sums / total_rows
     return (centered * lax.rsqrt(column_var + VAR_EPS)[None, :]).astype(jnp.bfloat16)
 

time: 206 us -> 194 us (0.942)
  blocking collectives: 67.7 us -> 55.4 us
    psum x1 -> x0, blocking collectives: 29.5 us -> none  [body(): square_sums = lax.psum(jnp.sum(centered * centered, axis=0), 'rows')]
    all_gather x0 -> x1, blocking collectives: none -> 17.2 us  [body(): lax.all_gather(jnp.sum(centered * centered, axis=0), 'rows')]
  transfers between devices with their start and end apart: 2 -> 2, of which waited for: 2 -> 2; matrix products, arithmetic and copies ran while one was open for 2% -> 3% of each run, Pallas kernels for 0% -> 0%
where the time goes in v1:
time: 194 us
  waiting for transfers between devices  100 us (52%)
  blocking collectives  55.4 us (29%)
  matrix products  14.7 us (8%)
  between operations  13.4 us (7%)
  other arithmetic  9.72 us (5%)
    all_gather x1, waiting for transfers between devices, body(): lax.all_gather(queries, 'rows', axis=0, tiled=True)  79.2 us
    psum x1, blocking collectives, body(): sums = lax.psum(jnp.sum(scored, axis=0), 'rows')  33 us
    reduce_scatter x1, waiting for transfers between devices, body(): lax.psum_scatter(partial_float.astype(jnp.bfloat16), 'feat', scatter_dime...  20.5 us
    all_gather x1, blocking collectives, body(): lax.all_gather(jnp.sum(centered * centered, axis=0), 'rows')  17.2 us
    dot_general x1, matrix products, body(): lax.dot_general(gradients, lax.all_gather(queries, 'rows', axis=0, tiled=...  14.7 us
    psum x1, blocking collectives, body(): squares = lax.psum(local_squares, 'feat')  5.15 us
    reduce_sum x1, other arithmetic, body(): local_squares = jnp.sum(jnp.square(gradients.astype(jnp.float32)), axis=1)  5.08 us
  transfers between devices with their start and end apart: 2, of which 2 were waited for; matrix products, arithmetic and copies ran while one was open for 3% of the time, Pallas kernels for 0%

profile of v1, /device:TPU:0, one launch (start us, length us, event | category | flops | bytes accessed | tf_op | source)
XLA Modules:
  0.0 193.8 jit_solution(1940195850533825410)
XLA Ops:
  6.5 0.0 all-gather.4.cloned.1.call-start
  6.5 0.7 all-gather.4.cloned.1.call-update
  7.3 0.0 reduce-scatter.2.cloned.1.call-start
  7.3 79.2 %all-gather.4.cloned.1.call-done = bf16[1024,4096]{1,0:T(8,128)(2,1)} async-done(((bf16[64,4096]{1,0:T(8,128)(2,1)}), bf16[1024,4096]{1,0:T(8,128)(2,1)}) %all-gather.4.cloned.1.call-update) | async-done | bytes 8388624 | tf_op jit(solution)/shard_map/all_gather | solution.py:18
  86.5 14.7 %convolution_convert_fusion = bf16[1024,1024]{1,0:T(8,128)(2,1)} fusion(bf16[1024,4096]{1,0:T(8,128)(2,1)} %param.3, bf16[1024,4096]{1,0:T(8,128)(2,1)} %all-gather.4.cloned.1.call-done), kind=kOutput, calls=%fused_computation.6 | convolution fusion | flops 8590983168 | bytes 18874368 | tf_op jit(solution)/shard_map/dot_general | solution.py:16
  101.3 0.0 reduce-scatter.2.cloned.1.call-update
  101.3 0.0 copy-start.1
  101.3 5.1 %multiply_reduce_fusion = f32[1024]{0:T(1024)S(1)} fusion(bf16[1024,4096]{1,0:T(8,128)(2,1)} %param.3), kind=kLoop, calls=%fused_computation | loop fusion | flops 12581888 | bytes 8392704 | tf_op jit(solution)/shard_map/reduce_sum | solution.py:14
  106.4 5.1 %psum.14 = f32[1024]{0:T(1024)S(1)} all-reduce(f32[1024]{0:T(1024)S(1)} %multiply_reduce_fusion), channel_id=1, replica_groups=mesh['rows'=16,'feat'=2] {'feat'}, use_global_device_ids=true, to_apply=%region_2.0 | all-reduce | flops 1024 | bytes 8192 | tf_op jit(solution)/shard_map/psum | solution.py:15
  111.5 0.0 copy-done.1
  111.6 20.5 %reduce-scatter.2.cloned.1.call-done = bf16[1024,512]{1,0:T(8,128)(2,1)} async-done(((bf16[1024,1024]{1,0:T(8,128)(2,1)}), bf16[1024,512]{1,0:T(8,128)(2,1)}) %reduce-scatter.2.cloned.1.call-update) | async-done | bytes 1048592 | tf_op jit(solution)/shard_map/reduce_scatter | solution.py:24
  132.1 0.0 copy-start
  132.1 1.6 fusion.1
  133.7 33.0 %psum.15 = f32[512]{0:T(512)S(1)} all-reduce(f32[512]{0:T(512)S(1)} %fusion.1), channel_id=1, replica_groups=mesh['rows'=16,'feat'=2] {'rows'}, use_global_device_ids=true, to_apply=%region_4.0 | all-reduce | flops 512 | bytes 4096 | tf_op jit(solution)/shard_map/psum | solution.py:29
  166.7 1.6 multiply_reduce_fusion.1
  168.3 17.2 %all-gather.1 = f32[16,1,512]{2,1,0:T(1,128)S(1)} all-gather(f32[1,1,512]{2,1,0:T(1,128)S(1)} %bitcast.3), channel_id=2, replica_groups=mesh['rows'=16,'feat'=2] {'rows'}, dimensions={0}, use_global_device_ids=true | all-gather | bytes 34816 | tf_op jit(solution)/shard_map/all_gather | solution.py:32
  185.6 0.0 copy-done
  185.6 1.3 multiply_convert_fusion
  (4 shorter events, 0.1 us)
Async XLA Ops:
  6.5 80.0 %all-gather.4.cloned.1.call-start = ((), (), s32[]{:S(2)}) async-start(), calls=%async_computation.1 | async-start | bytes 8912896 | tf_op jit(solution)/shard_map/all_gather | solution.py:18
  7.3 124.8 %reduce-scatter.2.cloned.1.call-start = ((), (), s32[]{:S(2)}) async-start(), calls=%async_computation.2 | async-start | bytes 3145728 | tf_op jit(solution)/shard_map/reduce_scatter | solution.py:24
  101.3 10.2 %copy-start.1 = (f32[1024]{0:T(1024)S(1)}, f32[1024]{0:T(1024)}, u32[]{:S(2)}) copy-start(f32[1024]{0:T(1024)} %param.5) | copy-start | bytes 12292
  132.1 53.6 %copy-start = (bf16[1024,512]{1,0:T(8,128)(2,1)S(1)}, bf16[1024,512]{1,0:T(8,128)(2,1)}, u32[]{:S(2)}) copy-start(bf16[1024,512]{1,0:T(8,128)(2,1)} %reduce-scatter.2.cloned.1.call-done) | copy-start | bytes 3145732
Sparse Core Ops, SparseCore 0:
  9.5 77.0 all-gather.3
  101.4 30.5 reduce-scatter.1
